TPU v7x, 32 devices: a whole 2x2x4 slice. The times are simulated.
32 devices in a mesh: grp: 2 (over x), col: 16 (over z, y, core).
Axes of the slice: x: 2, y: 2, z: 4, core: 2. Of those that a mesh axis runs over, the one named last changes fastest.
Arguments:
- mode_rows: float32 [16384, 256], P(('grp', 'col')), parts along dimension 0, may hold values from -8 to 8, as said below
- coeffs: bfloat16 [512, 256], P(('grp', 'col')), parts along dimension 0, may hold values from -18 to 18, as said below
- diffusivity: float32 [32, 64], P(('grp', 'col')), parts along dimension 0, may hold values from 0.02 to 0.24
- counts: int32 [32], P(('grp', 'col')), parts along dimension 0, may hold values from 32 to 64
- emis_idx: int32 [512], P('grp'), parts along dimension 0, may hold values from 0 to 15
- emis_table: float32 [16, 8], replicated, may hold values from 0.2 to 1.5
- reactants: int32 [12, 2], replicated, may hold values from 0 to 7
- stoich: int32 [12, 8], replicated, may hold values from -1 to 1
- rate_consts: float32 [12], replicated, may hold values from 0.02 to 0.2
- loss_rates: float32 [8], replicated, may hold values from 0.2 to 2
Outputs:
- modes_out: float32 [16384, 256], P(('grp', 'col')), parts along dimension 0
- coeffs_out: bfloat16 [512, 256], P(('grp', 'col')), parts along dimension 0
There are 2 independent parts, one for each index of `grp`. A program takes and returns all parts, laid end to end along the dimension named above; an argument that names none is the same for every part. Nothing has to cross between parts.
Inputs may be any that keep to these rules, and one draw needn't show every extreme that they name: `mode_rows`: modes of order one. `coeffs`: coefficients of order one.
All inputs are finite; a program needn't handle non-finite values.
Results may differ from a plain program's by a relative error of at most 0.0014.
The roundings to bfloat16 on the way count: a program that leaves them out, or rounds other values in their place, can miss the bound.
Values may be sent and summed in bfloat16 or wider, within the bound.
No kernel may reach another device: no remote copies, remote signals or barrier semaphores. Data moves between devices by JAX's collectives and lax.ppermute only.
A program may use at most 64 MiB of HBM per device.

v0:
```python
import math
import jax
import jax.numpy as jnp
from jax import lax
from jax.sharding import PartitionSpec as P

S = 8
LEV = 64
R = 256
NEMIS = 16
NSUB = 2
TIME_STEP = 0.1
RATE_STEP = 0.3
RIDGE_SHARE = 0.05
PRECISE = lax.Precision.HIGHEST


def diffuse(mode_block, diffusivity, counts):
    ncols = counts.shape[0]
    rank = mode_block.shape[1]
    blocked = mode_block.reshape(ncols, S, LEV, rank)
    level_index = jnp.arange(LEV, dtype=jnp.int32)
    face_coef = jnp.where(
        level_index[None, :] + 1 < counts[:, None], diffusivity, jnp.zeros_like(diffusivity)
    )
    upper_cells = jnp.concatenate([blocked[:, :, 1:], jnp.zeros_like(blocked[:, :, :1])], axis=2)
    face_flux = face_coef[:, None, :, None] * (upper_cells - blocked)
    lower_flux = jnp.concatenate(
        [jnp.zeros_like(face_flux[:, :, :1]), face_flux[:, :, :-1]], axis=2
    )
    return (blocked + face_flux - lower_flux).reshape(mode_block.shape)


def species_pick(table_column):
    return (table_column[:, None] == jnp.arange(S, dtype=jnp.int32)[None, :]).astype(jnp.float32)


def reaction(
    field_block,
    pick_first,
    pick_second,
    stoich_wide,
    rate_consts,
    loss_rates,
    emis_block,
    active,
    profile,
):
    first_amount = jnp.einsum("rs,bcsl->bcrl", pick_first, field_block, precision=PRECISE)
    second_amount = jnp.einsum("rs,bcsl->bcrl", pick_second, field_block, precision=PRECISE)
    reaction_speed = rate_consts[None, None, :, None] * first_amount * second_amount
    produced = jnp.einsum("rs,bcrl->bcsl", stoich_wide, reaction_speed, precision=PRECISE)
    tendency_raw = (
        produced
        - loss_rates[None, None, :, None] * field_block
        + emis_block[:, None, :, None] * profile[None, None, None, :]
    )
    return tendency_raw * active[None, :, None, :]


def on_device(
    mode_rows,
    coeffs,
    diffusivity,
    counts,
    emis_idx,
    emis_table,
    reactants,
    stoich,
    rate_consts,
    loss_rates,
):
    rows_dev = mode_rows.shape[0]
    mem_dev = coeffs.shape[0]
    col_count = lax.axis_size("col")
    total_rows = rows_dev * col_count
    members = mem_dev * col_count
    columns_dev = counts.shape[0]
    level_index = jnp.arange(LEV, dtype=jnp.int32)
    active = (level_index[None, :] < counts[:, None]).astype(jnp.float32)
    profile = jnp.exp(-4.0 * level_index.astype(jnp.float32) / LEV)
    chosen = (emis_idx[:, None] == jnp.arange(NEMIS, dtype=jnp.int32)[None, :]).astype(jnp.float32)
    member_emis = jnp.sum(chosen[:, :, None] * emis_table[None, :, :], axis=1)
    pick_first = species_pick(reactants[:, 0])
    pick_second = species_pick(reactants[:, 1])
    stoich_wide = stoich.astype(jnp.float32)
    rank_root = math.sqrt(R)
    inv_root = 1.0 / rank_root
    block_rows = math.gcd(members, 128)
    block_count = members // block_rows
    modes = mode_rows
    for substep in range(NSUB):
        diffused = diffuse(modes, diffusivity, counts)
        mode_bf = diffused.astype(jnp.bfloat16)
        rate_scale = rank_root / total_rows
        coef_gathered = lax.all_gather(coeffs, "col", axis=0, tiled=True)

        def member_block(pulled, block_inputs):
            coef_block, emis_block = block_inputs
            field_block = (
                lax.dot_general(
                    coef_block,
                    mode_bf,
                    (((1,), (1,)), ((), ())),
                    preferred_element_type=jnp.float32,
                )
                * inv_root
            )
            tendency = reaction(
                field_block.reshape(block_rows, columns_dev, S, LEV),
                pick_first,
                pick_second,
                stoich_wide,
                rate_consts,
                loss_rates,
                emis_block,
                active,
                profile,
            )
            tendency = tendency.reshape(block_rows, rows_dev).astype(jnp.bfloat16)
            pulled = pulled + lax.dot_general(
                tendency, coef_block, (((0,), (0,)), ((), ())), preferred_element_type=jnp.float32
            )
            part_rate = jnp.dot(tendency, mode_bf, preferred_element_type=jnp.float32)
            return (pulled, part_rate)

        pulled, rate_blocks = lax.scan(
            member_block,
            jnp.zeros((rows_dev, R), jnp.float32),
            (
                coef_gathered.reshape(block_count, block_rows, R),
                member_emis.reshape(block_count, block_rows, S),
            ),
        )
        pulled, rate_term = (pulled, rate_blocks.reshape(members, R))
        rate_mine = lax.psum_scatter(rate_term, "col", scatter_dimension=0, tiled=True) * rate_scale
        coef_wide = coeffs.astype(jnp.float32)
        gram_part = jnp.dot(coef_wide.T, coef_wide, precision=PRECISE)
        proj_part = lax.dot_general(
            mode_bf.astype(jnp.float32), pulled, (((0,), (0,)), ((), ())), precision=PRECISE
        )
        gram_matrix, proj_matrix = lax.psum((gram_part, proj_part), "col")
        proj_matrix = proj_matrix / total_rows
        gram_matrix = gram_matrix + RIDGE_SHARE * members * jnp.eye(R, dtype=jnp.float32)
        remainder = pulled - jnp.dot(diffused, proj_matrix, precision=PRECISE)
        factor = jnp.linalg.cholesky(gram_matrix)
        solved = jax.scipy.linalg.cho_solve((factor, True), remainder.T).T
        modes = diffused + TIME_STEP * rank_root * solved
        coeffs = (coef_wide + RATE_STEP * rate_mine).astype(jnp.bfloat16)
    return (modes, coeffs)


def solution(mesh):
    placed = (
        P(("grp", "col"), None),
        P(("grp", "col"), None),
        P(("grp", "col"), None),
        P(("grp", "col")),
        P("grp"),
        P(),
        P(),
        P(),
        P(),
        P(),
    )
    return jax.shard_map(
        on_device,
        mesh=mesh,
        in_specs=placed,
        out_specs=(P(("grp", "col"), None), P(("grp", "col"), None)),
        check_vma=False,
    )
```

profile of v0, /device:TPU:1, one launch (start us, length us, event | category | flops | bytes accessed | tf_op | source)
XLA Modules:
  0.0 393.6 jit_solution(5223242467514382098)
XLA Ops:
  7.2 23.6 %all_gather.6 = bf16[256,256]{1,0:T(8,128)(2,1)S(1)} all-gather(bf16[16,256]{1,0:T(8,128)(2,1)} %param.18), channel_id=1, replica_groups=mesh['grp'=2,'col'=16] {'col'}, dimensions={0}, use_global_device_ids=true | all-gather | bytes 139264 | tf_op jit(solution)/shard_map/all_gather | solution.py:96
  31.7 1.2 slice.80
  38.0 7.1 %while.30 = (s32[]{:T(128)}, f32[512,256]{1,0:T(8,128)S(1)}, f32[2,128,256]{2,1,0:T(8,128)S(1)}, f32[12]{0:T(128)S(1)}, bf16[2,128,256]{2,1,0:T(8,128)(2,1)S(1)}...) while((s32[]{:T(128)}, f32[512,256]{1,0:T(8,128)S(1)}, ...), condition=%wide.region_7.9_spmd.clone, body=%wide.region_6.8_spmd.clone.sunk | while | flops 129892992 | bytes 5650131 | solution.py:127
  45.1 1.2 fusion.103
  47.7 86.4 %all-reduce.12.cloned.1.call-done = (f32[256,256]{1,0:T(8,128)}, f32[256,256]{0,1:T(8,128)}) async-done(((f32[256,256]{1,0:T(8,128)}, f32[256,256]{0,1:T(8,128)}), (f32[256,256]{1,0:T(8,128)}, f32[256,256]{0,1:T(8,128)})) %all-reduce.12.cloned.1.call-update) | async-done | bytes 524304 | tf_op jit(solution)/shard_map/psum | solution.py:142
  136.1 11.7 %cholesky.130 = f32[128,128]{1,0:T(8,128)S(1)} custom-call(f32[128,128]{1,0:T(8,128)S(1)} %cholesky.194), custom_call_target="Cholesky" | custom-call | tf_op jit(solution)/shard_map/jit(cholesky)/cholesky | solution.py:146
  147.8 9.8 %custom-call.17 = f32[1,128,128]{1,2,0:T(8,128)S(1)} custom-call(f32[1,128,128]{2,1,0:T(8,128)S(1)} %get-tuple-element.369), custom_call_target="InvertDiagBlocksLowerTriangular" | custom-call | tf_op jit(solution)/shard_map/jit(cholesky)/cholesky | solution.py:146
  158.1 11.7 %cholesky.147 = f32[128,128]{1,0:T(8,128)S(1)} custom-call(f32[128,128]{1,0:T(8,128)S(1)} %convolution_subtract_fusion.7), custom_call_target="Cholesky" | custom-call | tf_op jit(solution)/shard_map/jit(cholesky)/cholesky | solution.py:146
  171.9 4.4 %while.32 = (s32[]{:T(128)}, f32[256,256]{1,0:T(8,128)S(1)}, s32[2,2]{1,0:T(2,128)S(1)}, f32[2,128,128]{2,1,0:T(8,128)S(1)}, s32[]{:T(128)}) while((s32[]{:T(128)}, f32[256,256]{1,0:T(8,128)S(1)}, s32[2,2]{1,0:T(2,128)S(1)}, f32[2,128,128]{2,1,0:T(8,128)S(1)}, s32[]{:T(128)}) %tuple.90), condition=%wide.while_cond, body=%wide.while_body.sunk | while | flops 2 | bytes 131181 | solution.py:147
  173.0 1.3 bitcast_dynamic-update-slice_fusion.4
  174.9 1.3 bitcast_dynamic-update-slice_fusion.4
  176.2 19.7 %custom-call.18 = f32[2,128,128]{1,2,0:T(8,128)S(1)} custom-call(f32[2,128,128]{2,1,0:T(8,128)S(1)} %get-tuple-element.258), custom_call_target="InvertDiagBlocksLowerTriangular" | custom-call | tf_op jit(solution)/shard_map/jit(_cho_solve)/triangular_solve | solution.py:147
  200.6 21.0 %all_gather.7 = bf16[256,256]{1,0:T(8,128)(2,1)S(1)} all-gather(bf16[16,256]{1,0:T(8,128)(2,1)S(1)} %add_convert_fusion.1), channel_id=1, replica_groups=mesh['grp'=2,'col'=16] {'col'}, dimensions={0}, use_global_device_ids=true | all-gather | bytes 139264 | tf_op jit(solution)/shard_map/all_gather | solution.py:96
  222.6 7.1 %while.31 = (s32[]{:T(128)}, f32[512,256]{1,0:T(8,128)S(1)}, f32[2,128,256]{2,1,0:T(8,128)S(1)}, f32[12]{0:T(128)S(1)}, bf16[2,128,256]{2,1,0:T(8,128)(2,1)S(1)}...) while((s32[]{:T(128)}, f32[512,256]{1,0:T(8,128)S(1)}, ...), condition=%wide.region_12.15_spmd.clone, body=%wide.region_11.14_spmd.clone.sunk | while | flops 129892992 | bytes 5650131 | solution.py:127
  229.7 1.2 fusion.105
  231.5 87.1 %all-reduce.10.cloned.1.call-done = (f32[256,256]{1,0:T(8,128)}, f32[256,256]{0,1:T(8,128)}) async-done(((f32[256,256]{1,0:T(8,128)}, f32[256,256]{0,1:T(8,128)}), (f32[256,256]{1,0:T(8,128)}, f32[256,256]{0,1:T(8,128)})) %all-reduce.10.cloned.1.call-update) | async-done | bytes 524304 | tf_op jit(solution)/shard_map/psum | solution.py:142
  320.6 11.7 %cholesky.164 = f32[128,128]{1,0:T(8,128)S(1)} custom-call(f32[128,128]{1,0:T(8,128)S(1)} %cholesky.197), custom_call_target="Cholesky" | custom-call | tf_op jit(solution)/shard_map/jit(cholesky)/cholesky | solution.py:146
  332.4 9.8 %custom-call.19 = f32[1,128,128]{1,2,0:T(8,128)S(1)} custom-call(f32[1,128,128]{2,1,0:T(8,128)S(1)} %get-tuple-element.365), custom_call_target="InvertDiagBlocksLowerTriangular" | custom-call | tf_op jit(solution)/shard_map/jit(cholesky)/cholesky | solution.py:146
  342.7 11.7 %cholesky.181 = f32[128,128]{1,0:T(8,128)S(1)} custom-call(f32[128,128]{1,0:T(8,128)S(1)} %convolution_subtract_fusion.6), custom_call_target="Cholesky" | custom-call | tf_op jit(solution)/shard_map/jit(cholesky)/cholesky | solution.py:146
  357.2 4.3 %while.33 = (s32[]{:T(128)}, f32[256,256]{1,0:T(8,128)S(1)}, s32[2,2]{1,0:T(2,128)S(1)}, f32[2,128,128]{2,1,0:T(8,128)S(1)}, s32[]{:T(128)}) while((s32[]{:T(128)}, f32[256,256]{1,0:T(8,128)S(1)}, s32[2,2]{1,0:T(2,128)S(1)}, f32[2,128,128]{2,1,0:T(8,128)S(1)}, s32[]{:T(128)}) %tuple.120), condition=%wide.while_cond.clone, body=%wide.while_body.clone.sunk | while | flops 2 | bytes 131181 | solution.py:147
  358.0 1.4 bitcast_dynamic-update-slice_fusion.5
  360.1 1.4 bitcast_dynamic-update-slice_fusion.5
  361.5 19.7 %custom-call.20 = f32[2,128,128]{1,2,0:T(8,128)S(1)} custom-call(f32[2,128,128]{2,1,0:T(8,128)S(1)} %get-tuple-element.259), custom_call_target="InvertDiagBlocksLowerTriangular" | custom-call | tf_op jit(solution)/shard_map/jit(_cho_solve)/triangular_solve | solution.py:147
  385.5 1.3 add_convert_fusion
  (159 shorter events, 40.4 us)
Async XLA Ops:
  7.2 126.9 %all-reduce.12.cloned.1.call-start = ((), (), s32[]{:S(2)}) async-start(), calls=%async_computation.5 | async-start | bytes 1048576 | tf_op jit(solution)/shard_map/psum | solution.py:142
  7.2 23.6 %copy-start.7 = (bf16[16,256]{1,0:T(8,128)(2,1)S(1)}, bf16[16,256]{1,0:T(8,128)(2,1)}, u32[]{:S(2)}) copy-start(bf16[16,256]{1,0:T(8,128)(2,1)} %param.18) | copy-start | bytes 24580
  31.7 2.5 copy-start
  33.6 0.7 copy-start.14
  34.5 0.7 copy-start.13
  35.2 0.7 copy-start.12
  35.9 0.7 copy-start.10
  36.6 0.7 copy-start.11
  37.4 0.7 copy-start.8
  37.4 0.7 copy-start.9
  45.1 1.2 copy-start.3
  46.3 153.5 %reduce-scatter.3.cloned.1.call-start = ((), (), s32[]{:S(2)}) async-start(), calls=%async_computation.2 | async-start | bytes 278528 | tf_op jit(solution)/shard_map/reduce_scatter | solution.py:136
  47.1 271.5 %all-reduce.10.cloned.1.call-start = ((), (), s32[]{:S(2)}) async-start(), calls=%async_computation.4 | async-start | bytes 1048576 | tf_op jit(solution)/shard_map/psum | solution.py:142
  135.1 1.0 copy-start.1
  171.9 24.1 %copy-start.5 = (f32[256,256]{1,0:T(8,128)S(1)}, f32[256,256]{1,0:T(8,128)}, u32[]{:S(2)}) copy-start(f32[256,256]{1,0:T(8,128)} %get-tuple-element.356) | copy-start | bytes 786436
  229.7 1.2 copy-start.4
  230.9 154.6 %reduce-scatter.5.cloned.1.call-start = ((), (), s32[]{:S(2)}) async-start(), calls=%async_computation.3 | async-start | bytes 278528 | tf_op jit(solution)/shard_map/reduce_scatter | solution.py:136
  319.6 1.0 copy-start.2
  357.2 24.0 %copy-start.6 = (f32[256,256]{1,0:T(8,128)S(1)}, f32[256,256]{1,0:T(8,128)}, u32[]{:S(2)}) copy-start(f32[256,256]{1,0:T(8,128)} %get-tuple-element.354) | copy-start | bytes 786436
Sparse Core Ops, SparseCore 0:
  46.5 87.5 all-reduce.11
  137.6 53.6 reduce-scatter.2
  231.0 87.5 all-reduce.9
  322.0 53.5 reduce-scatter.4
where the time goes:
time: 398 us; the launch traced here: 394 us
  waiting for transfers between devices  174 us (44%)
  other arithmetic  116 us (29%)
  blocking collectives  44.6 us (11%)
  matrix products  22 us (6%)
  between operations  17.7 us (4%)
  local copies, waits for them, and re-layouts  17.3 us (4%)
    psum x2, waiting for transfers between devices, on_device(): gram_matrix, proj_matrix = lax.psum((gram_part, proj_part), 'col')  174 us
    another operation x13, other arithmetic, on_device(): factor = jnp.linalg.cholesky(gram_matrix)  68.6 us
    all_gather x2, blocking collectives, on_device(): coef_gathered = lax.all_gather(coeffs, 'col', axis=0, tiled=True)  44.6 us
    another operation x5, other arithmetic, on_device(): solved = jax.scipy.linalg.cho_solve((factor, True), remainder.T).T  39.4 us
  transfers between devices with their start and end apart: 4, of which 2 were waited for; matrix products, arithmetic and copies ran while one was open for 32% of the time, Pallas kernels for 0%

commit v1 on v0

--- a/solution.py
+++ b/solution.py
@@ -13,6 +13,14 @@
 RATE_STEP = 0.3
 RIDGE_SHARE = 0.05
 PRECISE = lax.Precision.HIGHEST
+
+
+def series_unite(x0, axis_no):
+    x0 = jnp.moveaxis(x0, 0, axis_no)
+    block_now = x0.shape
+    return x0.reshape(
+        *block_now[:axis_no], block_now[axis_no] * block_now[axis_no + 1], *block_now[axis_no + 2 :]
+    )
 
 
 def diffuse(mode_block, diffusivity, counts):
@@ -93,7 +101,23 @@
         diffused = diffuse(modes, diffusivity, counts)
         mode_bf = diffused.astype(jnp.bfloat16)
         rate_scale = rank_root / total_rows
-        coef_gathered = lax.all_gather(coeffs, "col", axis=0, tiled=True)
+        shares = lax.axis_size("col")
+        buffer = [(i0, (i0 + 1) % shares) for i0 in range(shares)]
+        store = [(b, q) for q, b in buffer]
+        d_next, frame_out = ([], [])
+        for u in range(shares - 1):
+            if u % 2 == 0:
+                z2 = lax.ppermute(d_next[-1] if d_next else coeffs, "col", buffer)
+                d_next.append(z2)
+            else:
+                main = lax.ppermute(frame_out[-1] if frame_out else coeffs, "col", store)
+                frame_out.append(main)
+        prior = jnp.stack([*d_next[::-1], coeffs, *frame_out])
+        then = len(d_next)
+        oldest = lax.axis_index("col")
+        field_out = oldest - then
+        prior = prior[(jnp.arange(shares) - field_out) % shares]
+        coef_gathered = series_unite(prior, 0)
 
         def member_block(pulled, block_inputs):
             coef_block, emis_block = block_inputs

time: 398 us -> 450 us (1.13)
  starting transfers between devices: 0.62 us -> 70 us
  blocking collectives: 44.6 us -> 0 us
  waiting for transfers between devices: 174 us -> 203 us
    ppermute x0 -> x30, starting transfers between devices: none -> 69.1 us  [the longest x14 61 us: on_device(): main = lax.ppermute(frame_out[-1] if frame_out else coeffs, 'col', store)]
    all_gather x2 -> x0, blocking collectives: 44.6 us -> none  [on_device(): coef_gathered = lax.all_gather(coeffs, 'col', axis=0, tiled=True)]
    psum x2, waiting for transfers between devices: 174 us -> 191 us  [on_device(): gram_matrix, proj_matrix = lax.psum((gram_part, proj_part), 'col')]
    ppermute x0 -> x30, waiting for transfers between devices: none -> 10.9 us  [the longest x14 7.54 us: on_device(): main = lax.ppermute(frame_out[-1] if frame_out else coeffs, 'col', store)]
  transfers between devices with their start and end apart: 4 -> 34, of which waited for: 2 -> 22; matrix products, arithmetic and copies ran while one was open for 32% -> 30% of each run, Pallas kernels for 0% -> 0%
where the time goes in v1:
time: 450 us; the launch traced here: 445 us
  waiting for transfers between devices  203 us (45%)
  other arithmetic  116 us (26%)
  starting transfers between devices  70 us (16%)
  matrix products  22 us (5%)
  between operations  18.2 us (4%)
  local copies, waits for them, and re-layouts  16.1 us (4%)
    psum x2, waiting for transfers between devices, on_device(): gram_matrix, proj_matrix = lax.psum((gram_part, proj_part), 'col')  191 us
    another operation x13, other arithmetic, on_device(): factor = jnp.linalg.cholesky(gram_matrix)  68.7 us
    ppermute x14, starting transfers between devices, on_device(): main = lax.ppermute(frame_out[-1] if frame_out else coeffs, 'col', store)  61 us
    another operation x5, other arithmetic, on_device(): solved = jax.scipy.linalg.cho_solve((factor, True), remainder.T).T  39.4 us
  transfers between devices with their start and end apart: 34, of which 22 were waited for; matrix products, arithmetic and copies ran while one was open for 30% of the time, Pallas kernels for 0%

profile of v1, /device:TPU:1, one launch (start us, length us, event | category | flops | bytes accessed | tf_op | source)
XLA Modules:
  0.0 445.5 jit_solution(14666413045978697926)
XLA Ops:
  23.2 5.0 %collective-permute-start.10 = (bf16[16,256]{1,0:T(8,128)(2,1)S(1)}, bf16[16,256]{1,0:T(8,128)(2,1)S(1)}, u32[]{:S(2)}, u32[]{:S(2)}) collective-permute-start(bf16[16,256]{1,0:T(8,128)(2,1)S(1)} %collective-permute-done.9), channel_id=1, source_target_pairs={{1,0},{2,1},{3,2},{4,3},{5,4},{6,5},{7,6},{8,7},{9,8},{10,9},{11,1... | collective-permute-start | bytes 24584 | tf_op jit(solution)/shard_map/ppermute | solution.py:113
  29.0 4.9 %collective-permute-start.11 = (bf16[16,256]{1,0:T(8,128)(2,1)S(1)}, bf16[16,256]{1,0:T(8,128)(2,1)S(1)}, u32[]{:S(2)}, u32[]{:S(2)}) collective-permute-start(bf16[16,256]{1,0:T(8,128)(2,1)S(1)} %collective-permute-done.10), channel_id=1, source_target_pairs={{1,0},{2,1},{3,2},{4,3},{5,4},{6,5},{7,6},{8,7},{9,8},{10,9},{11,1... | collective-permute-start | bytes 24584 | tf_op jit(solution)/shard_map/ppermute | solution.py:113
  34.8 4.9 %collective-permute-start.12 = (bf16[16,256]{1,0:T(8,128)(2,1)S(1)}, bf16[16,256]{1,0:T(8,128)(2,1)S(1)}, u32[]{:S(2)}, u32[]{:S(2)}) collective-permute-start(bf16[16,256]{1,0:T(8,128)(2,1)S(1)} %collective-permute-done.11), channel_id=1, source_target_pairs={{1,0},{2,1},{3,2},{4,3},{5,4},{6,5},{7,6},{8,7},{9,8},{10,9},{11,1... | collective-permute-start | bytes 24584 | tf_op jit(solution)/shard_map/ppermute | solution.py:113
  40.5 4.9 %collective-permute-start.13 = (bf16[16,256]{1,0:T(8,128)(2,1)S(1)}, bf16[16,256]{1,0:T(8,128)(2,1)S(1)}, u32[]{:S(2)}, u32[]{:S(2)}) collective-permute-start(bf16[16,256]{1,0:T(8,128)(2,1)S(1)} %collective-permute-done.12), channel_id=1, source_target_pairs={{1,0},{2,1},{3,2},{4,3},{5,4},{6,5},{7,6},{8,7},{9,8},{10,9},{11,1... | collective-permute-start | bytes 24584 | tf_op jit(solution)/shard_map/ppermute | solution.py:113
  46.3 4.9 %collective-permute-start.14 = (bf16[16,256]{1,0:T(8,128)(2,1)S(1)}, bf16[16,256]{1,0:T(8,128)(2,1)S(1)}, u32[]{:S(2)}, u32[]{:S(2)}) collective-permute-start(bf16[16,256]{1,0:T(8,128)(2,1)S(1)} %collective-permute-done.13), channel_id=1, source_target_pairs={{1,0},{2,1},{3,2},{4,3},{5,4},{6,5},{7,6},{8,7},{9,8},{10,9},{11,1... | collective-permute-start | bytes 24584 | tf_op jit(solution)/shard_map/ppermute | solution.py:113
  53.3 7.1 %while.30 = (s32[]{:T(128)}, f32[512,256]{1,0:T(8,128)S(1)}, f32[2,128,256]{2,1,0:T(8,128)S(1)}, f32[12]{0:T(128)S(1)}, bf16[2,128,256]{2,1,0:T(8,128)(2,1)S(1)}...) while((s32[]{:T(128)}, f32[512,256]{1,0:T(8,128)S(1)}, ...), condition=%wide.region_7.9_spmd.clone, body=%wide.region_6.8_spmd.clone.sunk | while | flops 129892992 | bytes 5650131 | solution.py:151
  63.0 95.4 %all-reduce.12.cloned.1.call-done = (f32[256,256]{1,0:T(8,128)}, f32[256,256]{0,1:T(8,128)}) async-done(((f32[256,256]{1,0:T(8,128)}, f32[256,256]{0,1:T(8,128)}), (f32[256,256]{1,0:T(8,128)}, f32[256,256]{0,1:T(8,128)})) %all-reduce.12.cloned.1.call-update) | async-done | bytes 524304 | tf_op jit(solution)/shard_map/psum | solution.py:166
  160.4 11.7 %cholesky.130 = f32[128,128]{1,0:T(8,128)S(1)} custom-call(f32[128,128]{1,0:T(8,128)S(1)} %cholesky.194), custom_call_target="Cholesky" | custom-call | tf_op jit(solution)/shard_map/jit(cholesky)/cholesky | solution.py:170
  172.1 9.8 %custom-call.17 = f32[1,128,128]{1,2,0:T(8,128)S(1)} custom-call(f32[1,128,128]{2,1,0:T(8,128)S(1)} %get-tuple-element.369), custom_call_target="InvertDiagBlocksLowerTriangular" | custom-call | tf_op jit(solution)/shard_map/jit(cholesky)/cholesky | solution.py:170
  182.4 11.7 %cholesky.147 = f32[128,128]{1,0:T(8,128)S(1)} custom-call(f32[128,128]{1,0:T(8,128)S(1)} %convolution_subtract_fusion.7), custom_call_target="Cholesky" | custom-call | tf_op jit(solution)/shard_map/jit(cholesky)/cholesky | solution.py:170
  200.6 19.7 %custom-call.18 = f32[2,128,128]{1,2,0:T(8,128)S(1)} custom-call(f32[2,128,128]{2,1,0:T(8,128)S(1)} %get-tuple-element.258), custom_call_target="InvertDiagBlocksLowerTriangular" | custom-call | tf_op jit(solution)/shard_map/jit(_cho_solve)/triangular_solve | solution.py:171
  230.2 5.0 %collective-permute-start.24 = (bf16[16,256]{1,0:T(8,128)(2,1)S(1)}, bf16[16,256]{1,0:T(8,128)(2,1)S(1)}, u32[]{:S(2)}, u32[]{:S(2)}) collective-permute-start(bf16[16,256]{1,0:T(8,128)(2,1)S(1)} %collective-permute-done.23), channel_id=1, source_target_pairs={{1,0},{2,1},{3,2},{4,3},{5,4},{6,5},{7,6},{8,7},{9,8},{10,9},{11,1... | collective-permute-start | bytes 24584 | tf_op jit(solution)/shard_map/ppermute | solution.py:113
  236.0 4.9 %collective-permute-start.25 = (bf16[16,256]{1,0:T(8,128)(2,1)S(1)}, bf16[16,256]{1,0:T(8,128)(2,1)S(1)}, u32[]{:S(2)}, u32[]{:S(2)}) collective-permute-start(bf16[16,256]{1,0:T(8,128)(2,1)S(1)} %collective-permute-done.24), channel_id=1, source_target_pairs={{1,0},{2,1},{3,2},{4,3},{5,4},{6,5},{7,6},{8,7},{9,8},{10,9},{11,1... | collective-permute-start | bytes 24584 | tf_op jit(solution)/shard_map/ppermute | solution.py:113
  241.7 4.9 %collective-permute-start.26 = (bf16[16,256]{1,0:T(8,128)(2,1)S(1)}, bf16[16,256]{1,0:T(8,128)(2,1)S(1)}, u32[]{:S(2)}, u32[]{:S(2)}) collective-permute-start(bf16[16,256]{1,0:T(8,128)(2,1)S(1)} %collective-permute-done.25), channel_id=1, source_target_pairs={{1,0},{2,1},{3,2},{4,3},{5,4},{6,5},{7,6},{8,7},{9,8},{10,9},{11,1... | collective-permute-start | bytes 24584 | tf_op jit(solution)/shard_map/ppermute | solution.py:113
  247.5 4.9 %collective-permute-start.27 = (bf16[16,256]{1,0:T(8,128)(2,1)S(1)}, bf16[16,256]{1,0:T(8,128)(2,1)S(1)}, u32[]{:S(2)}, u32[]{:S(2)}) collective-permute-start(bf16[16,256]{1,0:T(8,128)(2,1)S(1)} %collective-permute-done.26), channel_id=1, source_target_pairs={{1,0},{2,1},{3,2},{4,3},{5,4},{6,5},{7,6},{8,7},{9,8},{10,9},{11,1... | collective-permute-start | bytes 24584 | tf_op jit(solution)/shard_map/ppermute | solution.py:113
  253.3 4.9 %collective-permute-start.28 = (bf16[16,256]{1,0:T(8,128)(2,1)S(1)}, bf16[16,256]{1,0:T(8,128)(2,1)S(1)}, u32[]{:S(2)}, u32[]{:S(2)}) collective-permute-start(bf16[16,256]{1,0:T(8,128)(2,1)S(1)} %collective-permute-done.27), channel_id=1, source_target_pairs={{1,0},{2,1},{3,2},{4,3},{5,4},{6,5},{7,6},{8,7},{9,8},{10,9},{11,1... | collective-permute-start | bytes 24584 | tf_op jit(solution)/shard_map/ppermute | solution.py:113
  259.3 5.1 %collective-permute-start.29 = (bf16[16,256]{1,0:T(8,128)(2,1)S(1)}, bf16[16,256]{1,0:T(8,128)(2,1)S(1)}, u32[]{:S(2)}, u32[]{:S(2)}) collective-permute-start(bf16[16,256]{1,0:T(8,128)(2,1)S(1)} %collective-permute-done.28), channel_id=1, source_target_pairs={{1,0},{2,1},{3,2},{4,3},{5,4},{6,5},{7,6},{8,7},{9,8},{10,9},{11,1... | collective-permute-start | bytes 24584 | tf_op jit(solution)/shard_map/ppermute | solution.py:113
  265.8 7.1 %while.31 = (s32[]{:T(128)}, f32[512,256]{1,0:T(8,128)S(1)}, f32[2,128,256]{2,1,0:T(8,128)S(1)}, f32[12]{0:T(128)S(1)}, bf16[2,128,256]{2,1,0:T(8,128)(2,1)S(1)}...) while((s32[]{:T(128)}, f32[512,256]{1,0:T(8,128)S(1)}, ...), condition=%wide.region_12.15_spmd.clone, body=%wide.region_11.14_spmd.clone.sunk | while | flops 129892992 | bytes 5650131 | solution.py:151
  274.7 95.8 %all-reduce.10.cloned.1.call-done = (f32[256,256]{1,0:T(8,128)}, f32[256,256]{0,1:T(8,128)}) async-done(((f32[256,256]{1,0:T(8,128)}, f32[256,256]{0,1:T(8,128)}), (f32[256,256]{1,0:T(8,128)}, f32[256,256]{0,1:T(8,128)})) %all-reduce.10.cloned.1.call-update) | async-done | bytes 524304 | tf_op jit(solution)/shard_map/psum | solution.py:166
  372.5 11.7 %cholesky.164 = f32[128,128]{1,0:T(8,128)S(1)} custom-call(f32[128,128]{1,0:T(8,128)S(1)} %cholesky.197), custom_call_target="Cholesky" | custom-call | tf_op jit(solution)/shard_map/jit(cholesky)/cholesky | solution.py:170
  384.3 9.8 %custom-call.19 = f32[1,128,128]{1,2,0:T(8,128)S(1)} custom-call(f32[1,128,128]{2,1,0:T(8,128)S(1)} %get-tuple-element.365), custom_call_target="InvertDiagBlocksLowerTriangular" | custom-call | tf_op jit(solution)/shard_map/jit(cholesky)/cholesky | solution.py:170
  394.5 11.7 %cholesky.181 = f32[128,128]{1,0:T(8,128)S(1)} custom-call(f32[128,128]{1,0:T(8,128)S(1)} %convolution_subtract_fusion.6), custom_call_target="Cholesky" | custom-call | tf_op jit(solution)/shard_map/jit(cholesky)/cholesky | solution.py:170
  409.0 4.3 while.33
  413.3 19.7 %custom-call.20 = f32[2,128,128]{1,2,0:T(8,128)S(1)} custom-call(f32[2,128,128]{2,1,0:T(8,128)S(1)} %get-tuple-element.259), custom_call_target="InvertDiagBlocksLowerTriangular" | custom-call | tf_op jit(solution)/shard_map/jit(_cho_solve)/triangular_solve | solution.py:171
  (253 shorter events, 79.0 us)
Async XLA Ops:
  7.2 151.2 %all-reduce.12.cloned.1.call-start = ((), (), s32[]{:S(2)}) async-start(), calls=%async_computation.5 | async-start | bytes 1048576 | tf_op jit(solution)/shard_map/psum | solution.py:166
  9.9 8.6 %collective-permute-start.8 = (bf16[16,256]{1,0:T(8,128)(2,1)}, bf16[16,256]{1,0:T(8,128)(2,1)S(1)}, u32[]{:S(2)}, u32[]{:S(2)}) collective-permute-start(bf16[16,256]{1,0:T(8,128)(2,1)} %param.18), channel_id=1, source_target_pairs={{1,0},{2,1},{3,2},{4,3},{5,4},{6,5},{7,6},{8,7},{9,8},{10,9},{11,1... | collective-permute-start | bytes 24584 | tf_op jit(solution)/shard_map/ppermute | solution.py:113
  16.3 6.0 %collective-permute-start.2 = (bf16[16,256]{1,0:T(8,128)(2,1)S(1)}, bf16[16,256]{1,0:T(8,128)(2,1)S(1)}, u32[]{:S(2)}, u32[]{:S(2)}) collective-permute-start(bf16[16,256]{1,0:T(8,128)(2,1)S(1)} %collective-permute-done.1), channel_id=1, source_target_pairs={{0,1},{1,2},{2,3},{3,4},{4,5},{5,6},{6,7},{7,8},{8,9},{9,10},{10,1... | collective-permute-start | bytes 24584 | tf_op jit(solution)/shard_map/ppermute | solution.py:110
  22.4 5.8 %collective-permute-start.3 = (bf16[16,256]{1,0:T(8,128)(2,1)S(1)}, bf16[16,256]{1,0:T(8,128)(2,1)S(1)}, u32[]{:S(2)}, u32[]{:S(2)}) collective-permute-start(bf16[16,256]{1,0:T(8,128)(2,1)S(1)} %collective-permute-done.2), channel_id=1, source_target_pairs={{0,1},{1,2},{2,3},{3,4},{4,5},{5,6},{6,7},{7,8},{8,9},{9,10},{10,1... | collective-permute-start | bytes 24584 | tf_op jit(solution)/shard_map/ppermute | solution.py:110
  23.2 5.8 %collective-permute-start.10 = (bf16[16,256]{1,0:T(8,128)(2,1)S(1)}, bf16[16,256]{1,0:T(8,128)(2,1)S(1)}, u32[]{:S(2)}, u32[]{:S(2)}) collective-permute-start(bf16[16,256]{1,0:T(8,128)(2,1)S(1)} %collective-permute-done.9), channel_id=1, source_target_pairs={{1,0},{2,1},{3,2},{4,3},{5,4},{6,5},{7,6},{8,7},{9,8},{10,9},{11,1... | collective-permute-start | bytes 24584 | tf_op jit(solution)/shard_map/ppermute | solution.py:113
  28.2 5.8 %collective-permute-start.4 = (bf16[16,256]{1,0:T(8,128)(2,1)S(1)}, bf16[16,256]{1,0:T(8,128)(2,1)S(1)}, u32[]{:S(2)}, u32[]{:S(2)}) collective-permute-start(bf16[16,256]{1,0:T(8,128)(2,1)S(1)} %collective-permute-done.3), channel_id=1, source_target_pairs={{0,1},{1,2},{2,3},{3,4},{4,5},{5,6},{6,7},{7,8},{8,9},{9,10},{10,1... | collective-permute-start | bytes 24584 | tf_op jit(solution)/shard_map/ppermute | solution.py:110
  29.0 5.8 %collective-permute-start.11 = (bf16[16,256]{1,0:T(8,128)(2,1)S(1)}, bf16[16,256]{1,0:T(8,128)(2,1)S(1)}, u32[]{:S(2)}, u32[]{:S(2)}) collective-permute-start(bf16[16,256]{1,0:T(8,128)(2,1)S(1)} %collective-permute-done.10), channel_id=1, source_target_pairs={{1,0},{2,1},{3,2},{4,3},{5,4},{6,5},{7,6},{8,7},{9,8},{10,9},{11,1... | collective-permute-start | bytes 24584 | tf_op jit(solution)/shard_map/ppermute | solution.py:113
  33.9 5.8 %collective-permute-start.5 = (bf16[16,256]{1,0:T(8,128)(2,1)S(1)}, bf16[16,256]{1,0:T(8,128)(2,1)S(1)}, u32[]{:S(2)}, u32[]{:S(2)}) collective-permute-start(bf16[16,256]{1,0:T(8,128)(2,1)S(1)} %collective-permute-done.4), channel_id=1, source_target_pairs={{0,1},{1,2},{2,3},{3,4},{4,5},{5,6},{6,7},{7,8},{8,9},{9,10},{10,1... | collective-permute-start | bytes 24584 | tf_op jit(solution)/shard_map/ppermute | solution.py:110
  34.8 5.8 %collective-permute-start.12 = (bf16[16,256]{1,0:T(8,128)(2,1)S(1)}, bf16[16,256]{1,0:T(8,128)(2,1)S(1)}, u32[]{:S(2)}, u32[]{:S(2)}) collective-permute-start(bf16[16,256]{1,0:T(8,128)(2,1)S(1)} %collective-permute-done.11), channel_id=1, source_target_pairs={{1,0},{2,1},{3,2},{4,3},{5,4},{6,5},{7,6},{8,7},{9,8},{10,9},{11,1... | collective-permute-start | bytes 24584 | tf_op jit(solution)/shard_map/ppermute | solution.py:113
  39.7 5.8 %collective-permute-start.6 = (bf16[16,256]{1,0:T(8,128)(2,1)S(1)}, bf16[16,256]{1,0:T(8,128)(2,1)S(1)}, u32[]{:S(2)}, u32[]{:S(2)}) collective-permute-start(bf16[16,256]{1,0:T(8,128)(2,1)S(1)} %collective-permute-done.5), channel_id=1, source_target_pairs={{0,1},{1,2},{2,3},{3,4},{4,5},{5,6},{6,7},{7,8},{8,9},{9,10},{10,1... | collective-permute-start | bytes 24584 | tf_op jit(solution)/shard_map/ppermute | solution.py:110
  40.5 5.8 %collective-permute-start.13 = (bf16[16,256]{1,0:T(8,128)(2,1)S(1)}, bf16[16,256]{1,0:T(8,128)(2,1)S(1)}, u32[]{:S(2)}, u32[]{:S(2)}) collective-permute-start(bf16[16,256]{1,0:T(8,128)(2,1)S(1)} %collective-permute-done.12), channel_id=1, source_target_pairs={{1,0},{2,1},{3,2},{4,3},{5,4},{6,5},{7,6},{8,7},{9,8},{10,9},{11,1... | collective-permute-start | bytes 24584 | tf_op jit(solution)/shard_map/ppermute | solution.py:113
  45.5 5.8 %collective-permute-start.7 = (bf16[16,256]{1,0:T(8,128)(2,1)S(1)}, bf16[16,256]{1,0:T(8,128)(2,1)S(1)}, u32[]{:S(2)}, u32[]{:S(2)}) collective-permute-start(bf16[16,256]{1,0:T(8,128)(2,1)S(1)} %collective-permute-done.6), channel_id=1, source_target_pairs={{0,1},{1,2},{2,3},{3,4},{4,5},{5,6},{6,7},{7,8},{8,9},{9,10},{10,1... | collective-permute-start | bytes 24584 | tf_op jit(solution)/shard_map/ppermute | solution.py:110
  46.3 5.8 %collective-permute-start.14 = (bf16[16,256]{1,0:T(8,128)(2,1)S(1)}, bf16[16,256]{1,0:T(8,128)(2,1)S(1)}, u32[]{:S(2)}, u32[]{:S(2)}) collective-permute-start(bf16[16,256]{1,0:T(8,128)(2,1)S(1)} %collective-permute-done.13), channel_id=1, source_target_pairs={{1,0},{2,1},{3,2},{4,3},{5,4},{6,5},{7,6},{8,7},{9,8},{10,9},{11,1... | collective-permute-start | bytes 24584 | tf_op jit(solution)/shard_map/ppermute | solution.py:113
  61.6 160.7 %reduce-scatter.3.cloned.1.call-start = ((), (), s32[]{:S(2)}) async-start(), calls=%async_computation.2 | async-start | bytes 278528 | tf_op jit(solution)/shard_map/reduce_scatter | solution.py:160
  62.4 308.1 %all-reduce.10.cloned.1.call-start = ((), (), s32[]{:S(2)}) async-start(), calls=%async_computation.4 | async-start | bytes 1048576 | tf_op jit(solution)/shard_map/psum | solution.py:166
  229.5 5.8 %collective-permute-start.17 = (bf16[16,256]{1,0:T(8,128)(2,1)S(1)}, bf16[16,256]{1,0:T(8,128)(2,1)S(1)}, u32[]{:S(2)}, u32[]{:S(2)}) collective-permute-start(bf16[16,256]{1,0:T(8,128)(2,1)S(1)} %collective-permute-done.16), channel_id=1, source_target_pairs={{0,1},{1,2},{2,3},{3,4},{4,5},{5,6},{6,7},{7,8},{8,9},{9,10},{10,1... | collective-permute-start | bytes 24584 | tf_op jit(solution)/shard_map/ppermute | solution.py:110
  230.2 5.8 %collective-permute-start.24 = (bf16[16,256]{1,0:T(8,128)(2,1)S(1)}, bf16[16,256]{1,0:T(8,128)(2,1)S(1)}, u32[]{:S(2)}, u32[]{:S(2)}) collective-permute-start(bf16[16,256]{1,0:T(8,128)(2,1)S(1)} %collective-permute-done.23), channel_id=1, source_target_pairs={{1,0},{2,1},{3,2},{4,3},{5,4},{6,5},{7,6},{8,7},{9,8},{10,9},{11,1... | collective-permute-start | bytes 24584 | tf_op jit(solution)/shard_map/ppermute | solution.py:113
  235.3 5.8 %collective-permute-start.18 = (bf16[16,256]{1,0:T(8,128)(2,1)S(1)}, bf16[16,256]{1,0:T(8,128)(2,1)S(1)}, u32[]{:S(2)}, u32[]{:S(2)}) collective-permute-start(bf16[16,256]{1,0:T(8,128)(2,1)S(1)} %collective-permute-done.17), channel_id=1, source_target_pairs={{0,1},{1,2},{2,3},{3,4},{4,5},{5,6},{6,7},{7,8},{8,9},{9,10},{10,1... | collective-permute-start | bytes 24584 | tf_op jit(solution)/shard_map/ppermute | solution.py:110
  236.0 5.8 %collective-permute-start.25 = (bf16[16,256]{1,0:T(8,128)(2,1)S(1)}, bf16[16,256]{1,0:T(8,128)(2,1)S(1)}, u32[]{:S(2)}, u32[]{:S(2)}) collective-permute-start(bf16[16,256]{1,0:T(8,128)(2,1)S(1)} %collective-permute-done.24), channel_id=1, source_target_pairs={{1,0},{2,1},{3,2},{4,3},{5,4},{6,5},{7,6},{8,7},{9,8},{10,9},{11,1... | collective-permute-start | bytes 24584 | tf_op jit(solution)/shard_map/ppermute | solution.py:113
  241.1 5.8 %collective-permute-start.19 = (bf16[16,256]{1,0:T(8,128)(2,1)S(1)}, bf16[16,256]{1,0:T(8,128)(2,1)S(1)}, u32[]{:S(2)}, u32[]{:S(2)}) collective-permute-start(bf16[16,256]{1,0:T(8,128)(2,1)S(1)} %collective-permute-done.18), channel_id=1, source_target_pairs={{0,1},{1,2},{2,3},{3,4},{4,5},{5,6},{6,7},{7,8},{8,9},{9,10},{10,1... | collective-permute-start | bytes 24584 | tf_op jit(solution)/shard_map/ppermute | solution.py:110
  253.3 6.0 %collective-permute-start.28 = (bf16[16,256]{1,0:T(8,128)(2,1)S(1)}, bf16[16,256]{1,0:T(8,128)(2,1)S(1)}, u32[]{:S(2)}, u32[]{:S(2)}) collective-permute-start(bf16[16,256]{1,0:T(8,128)(2,1)S(1)} %collective-permute-done.27), channel_id=1, source_target_pairs={{1,0},{2,1},{3,2},{4,3},{5,4},{6,5},{7,6},{8,7},{9,8},{10,9},{11,1... | collective-permute-start | bytes 24584 | tf_op jit(solution)/shard_map/ppermute | solution.py:113
  258.4 6.0 %collective-permute-start.22 = (bf16[16,256]{1,0:T(8,128)(2,1)S(1)}, bf16[16,256]{1,0:T(8,128)(2,1)S(1)}, u32[]{:S(2)}, u32[]{:S(2)}) collective-permute-start(bf16[16,256]{1,0:T(8,128)(2,1)S(1)} %collective-permute-done.21), channel_id=1, source_target_pairs={{0,1},{1,2},{2,3},{3,4},{4,5},{5,6},{6,7},{7,8},{8,9},{9,10},{10,1... | collective-permute-start | bytes 24584 | tf_op jit(solution)/shard_map/ppermute | solution.py:110
  259.3 5.9 %collective-permute-start.29 = (bf16[16,256]{1,0:T(8,128)(2,1)S(1)}, bf16[16,256]{1,0:T(8,128)(2,1)S(1)}, u32[]{:S(2)}, u32[]{:S(2)}) collective-permute-start(bf16[16,256]{1,0:T(8,128)(2,1)S(1)} %collective-permute-done.28), channel_id=1, source_target_pairs={{1,0},{2,1},{3,2},{4,3},{5,4},{6,5},{7,6},{8,7},{9,8},{10,9},{11,1... | collective-permute-start | bytes 24584 | tf_op jit(solution)/shard_map/ppermute | solution.py:113
  274.1 163.2 %reduce-scatter.5.cloned.1.call-start = ((), (), s32[]{:S(2)}) async-start(), calls=%async_computation.3 | async-start | bytes 278528 | tf_op jit(solution)/shard_map/reduce_scatter | solution.py:160
  (25 other events, 135.7 us)
Sparse Core Ops, SparseCore 0:
  61.7 96.5 all-reduce.11
  161.9 53.6 reduce-scatter.2
  274.3 96.1 all-reduce.9
  373.9 53.6 reduce-scatter.4
